TPU v7x, 256 devices: a whole 4x4x8 slice. The times are simulated.
256 devices in a mesh: chain: 64 (over z, y, core), col: 4 (over x).
Axes of the slice: x: 4, y: 4, z: 8, core: 2. Of those that a mesh axis runs over, the one named last changes fastest.
Arguments:
- diagonal_blocks: float32 [192, 256, 256], P('chain', 'col'), may hold values from -2 to 6, as said below
- couplings: float32 [192, 256, 256], P('chain', 'col'), may hold values from -2 to 2
- right_sides: float32 [64, 192, 256], P('col', 'chain'), may hold values from -0.04 to 0.04
Outputs:
- solution: float32 [64, 192, 256], P('col', 'chain')
Inputs may be any that keep to these rules, and one draw needn't show every extreme that they name: `diagonal_blocks`: each block is symmetric, and the block-tridiagonal matrix that the diagonal blocks form with the couplings is positive definite with every eigenvalue 0.0003 or more.
All inputs are finite; a program needn't handle non-finite values.
Results may differ from a plain program's by a relative error of at most 0.0003.
Values sent between devices are 32-bit elements; how exact they have to be, the bound alone decides.
A program may use at most 64 MiB of HBM per device.

v0:
```python
import jax
import jax.numpy as jnp
from jax import lax
from jax.sharding import PartitionSpec as P

finest = lax.Precision.HIGHEST


def passed_along(shard, axis, by):
    size = lax.axis_size(axis)
    pairs = [(i, i + by) for i in range(size) if 0 <= i + by < size]
    return lax.ppermute(shard, axis, pairs)


def matmul(first_factor, second_factor):
    return jnp.dot(first_factor, second_factor, precision=finest)


def invert(matrix):
    lower_factor = jnp.linalg.cholesky(matrix)
    identity = jnp.eye(matrix.shape[0], dtype=matrix.dtype)
    return jax.scipy.linalg.cho_solve((lower_factor, True), identity)


def interior_solve(loads, inverses, products, inner_coups):
    before = jnp.concatenate([jnp.zeros_like(inner_coups), inner_coups], axis=0)

    def interior_forward(solved_prev, entries):
        load_now, coup_prev, inverse_now = entries
        reduced = load_now - matmul(solved_prev, coup_prev)
        solved_now = matmul(reduced, inverse_now.T)
        return (solved_now, solved_now)

    _, solved = lax.scan(interior_forward, jnp.zeros_like(loads[0]), (loads, before, inverses))

    def interior_backward(after, entries):
        solved_now, product = entries
        current = solved_now - matmul(after, product.T)
        return (current, current)

    _, earlier = lax.scan(interior_backward, solved[-1], (solved[:-1], products), reverse=True)
    return jnp.concatenate([earlier, solved[-1:]], axis=0)


def per_device(diagonal_blocks, couplings, right_sides):
    slab_count = diagonal_blocks.shape[0]
    col_width = diagonal_blocks.shape[1]
    inner_count = slab_count - 1
    col_start = lax.axis_index("col") * col_width
    chain_count = lax.axis_size("chain")
    levels = chain_count.bit_length() - 1
    full_diag, full_coup = (
        lax.all_gather(diagonal_blocks[:inner_count], "col", axis=1, tiled=True),
        lax.all_gather(couplings, "col", axis=1, tiled=True),
    )

    def body_forward(inverse_prev, entries):
        diag_now, coup_prev = entries
        product = matmul(inverse_prev, coup_prev)
        inverse_now = invert(diag_now - matmul(coup_prev.T, product))
        return (inverse_now, (inverse_prev, product))

    last_inverse, (early_inverses, products) = lax.scan(
        body_forward, invert(full_diag[0]), (full_diag[1:], full_coup[: inner_count - 1])
    )
    inverses = jnp.concatenate([early_inverses, last_inverse[None]], axis=0)
    inner_coups = full_coup[: inner_count - 1]
    coup_last = full_coup[inner_count - 1]
    coup_sep = full_coup[inner_count]
    last_cols = lax.dynamic_slice_in_dim(coup_last, col_start, col_width, 1)
    tail_start = matmul(last_inverse, last_cols)

    def body_backward(state, entries):
        green_block, tail_block = state
        inverse_now, product = entries
        green_block = inverse_now + matmul(matmul(product, green_block), product.T)
        tail_block = -matmul(product, tail_block)
        return ((green_block, tail_block), None)

    (near_green, near_tail), _ = lax.scan(
        body_backward, (last_inverse, tail_start), (early_inverses, products), reverse=True
    )
    loads = jnp.swapaxes(right_sides, 0, 1)
    interior = interior_solve(loads[:inner_count], inverses, products, inner_coups)
    got_green, got_tail, got_first = passed_along((near_green, near_tail, interior[0]), "chain", -1)
    sep_rows = lax.dynamic_slice_in_dim(coup_sep, col_start, col_width, 0)
    own_block = diagonal_blocks[inner_count].T
    b_part = (
        own_block
        - matmul(coup_last.T, tail_start)
        - matmul(coup_sep, matmul(got_green, sep_rows.T))
    )
    c_part = -matmul(coup_sep, got_tail)
    h_part = (
        loads[inner_count]
        - matmul(interior[inner_count - 1], coup_last)
        - matmul(got_first, coup_sep.T)
    )
    for level_index in range(levels):
        distance = 1 << level_index
        b_full, c_full = (
            lax.all_gather(b_part, "col", axis=1, tiled=True),
            lax.all_gather(c_part, "col", axis=1, tiled=True),
        )
        inverse = invert(b_full)
        coupling_rows = lax.dynamic_slice_in_dim(c_full, col_start, col_width, 0)
        solved_cols = matmul(inverse, c_part)
        solved_loads = matmul(h_part, inverse.T)
        below_blocks, below_loads = passed_along(
            (matmul(c_full.T, solved_cols), matmul(solved_loads, c_full)), "chain", distance
        )
        far_inverse, far_cols, far_loads = passed_along(
            (inverse, solved_cols, solved_loads), "chain", -distance
        )
        b_part = b_part - below_blocks - matmul(c_full, matmul(far_inverse, coupling_rows.T))
        c_part = -matmul(c_full, far_cols)
        h_part = h_part - below_loads - matmul(far_loads, c_full.T)
    b_final = lax.all_gather(b_part, "col", axis=1, tiled=True)
    separator = jax.scipy.linalg.cho_solve((jnp.linalg.cholesky(b_final), True), h_part.T).T
    carried = passed_along(matmul(separator, coup_sep), "chain", 1)
    adjusted = loads[:inner_count]
    adjusted = adjusted.at[0].add(-carried)
    adjusted = adjusted.at[inner_count - 1].add(-matmul(separator, coup_last.T))
    solved_inner = interior_solve(adjusted, inverses, products, inner_coups)
    return jnp.swapaxes(jnp.concatenate([solved_inner, separator[None]], axis=0), 0, 1)


def solution(mesh):
    in_specs = (P("chain", "col", None), P("chain", "col", None), P("col", "chain", None))
    out_specs = P("col", "chain", None)
    return jax.shard_map(
        per_device, mesh=mesh, in_specs=in_specs, out_specs=out_specs, check_vma=False
    )
```

profile of v0, /device:TPU:250, one launch (start us, length us, event | category | flops | bytes accessed | tf_op | source)
XLA Modules:
  0.0 923.8 jit_solution(14875295477138087786)
XLA Ops:
  1.0 13.5 %all_gather.45 = f32[2,256,256]{2,0,1:T(2,128)S(1)} all-gather(f32[2,64,256]{2,0,1:T(2,128)S(1)} %copy.26), channel_id=1, replica_groups=mesh['chain'=64,'col'=4] {'col'}, dimensions={1}, use_global_device_ids=true | all-gather | bytes 655360 | tf_op jit(solution)/shard_map/all_gather | solution.py:53
  15.1 11.7 %cholesky.424 = f32[128,128]{1,0:T(8,128)S(1)} custom-call(f32[128,128]{1,0:T(8,128)S(1)} %cholesky.726), custom_call_target="Cholesky" | custom-call | tf_op jit(solution)/shard_map/jit(cholesky)/cholesky | solution.py:20
  26.9 9.8 %custom-call.36 = f32[1,128,128]{1,2,0:T(8,128)S(1)} custom-call(f32[1,128,128]{2,1,0:T(8,128)S(1)} %get-tuple-element.384), custom_call_target="InvertDiagBlocksLowerTriangular" | custom-call | tf_op jit(solution)/shard_map/jit(cholesky)/cholesky | solution.py:20
  37.2 11.7 %cholesky.441 = f32[128,128]{1,0:T(8,128)S(1)} custom-call(f32[128,128]{1,0:T(8,128)S(1)} %convolution_subtract_fusion.24), custom_call_target="Cholesky" | custom-call | tf_op jit(solution)/shard_map/jit(cholesky)/cholesky | solution.py:20
  55.0 19.7 %custom-call.37 = f32[2,128,128]{1,2,0:T(8,128)S(1)} custom-call(f32[2,128,128]{2,1,0:T(8,128)S(1)} %get-tuple-element.218), custom_call_target="InvertDiagBlocksLowerTriangular" | custom-call | tf_op jit(solution)/shard_map/jit(_cho_solve)/triangular_solve | solution.py:22
  77.1 14.0 %all_gather.46 = f32[3,256,256]{2,1,0:T(8,128)S(1)} all-gather(f32[3,64,256]{2,1,0:T(8,128)S(1)} %copy-done.19), channel_id=1, replica_groups=mesh['chain'=64,'col'=4] {'col'}, dimensions={1}, use_global_device_ids=true | all-gather | bytes 983040 | tf_op jit(solution)/shard_map/all_gather | solution.py:54
  93.3 11.7 %cholesky.458 = f32[128,128]{1,0:T(8,128)S(1)} custom-call(f32[128,128]{1,0:T(8,128)S(1)} %cholesky.729), custom_call_target="Cholesky" | custom-call | tf_op jit(solution)/shard_map/while/body/eval_jaxpr/jit(cholesky)/cholesky | solution.py:20
  105.0 9.8 %custom-call.38 = f32[1,128,128]{1,2,0:T(8,128)S(1)} custom-call(f32[1,128,128]{2,1,0:T(8,128)S(1)} %get-tuple-element.380), custom_call_target="InvertDiagBlocksLowerTriangular" | custom-call | tf_op jit(solution)/shard_map/while/body/eval_jaxpr/jit(cholesky)/cholesky | solution.py:20
  115.3 11.7 %cholesky.475 = f32[128,128]{1,0:T(8,128)S(1)} custom-call(f32[128,128]{1,0:T(8,128)S(1)} %convolution_subtract_fusion.23), custom_call_target="Cholesky" | custom-call | tf_op jit(solution)/shard_map/while/body/eval_jaxpr/jit(cholesky)/cholesky | solution.py:20
  133.8 19.7 %custom-call.39 = f32[2,128,128]{1,2,0:T(8,128)S(1)} custom-call(f32[2,128,128]{2,1,0:T(8,128)S(1)} %get-tuple-element.219), custom_call_target="InvertDiagBlocksLowerTriangular" | custom-call | tf_op jit(solution)/shard_map/while/body/eval_jaxpr/jit(_cho_solve)/triangular_solve | solution.py:22
  170.3 12.3 %all_gather.47 = f32[256,256]{0,1:T(8,128)S(1)} all-gather(f32[256,64]{0,1:T(8,128)S(1)} %bitcast.554), channel_id=1, replica_groups=mesh['chain'=64,'col'=4] {'col'}, dimensions={1}, use_global_device_ids=true | all-gather | bytes 327680 | tf_op jit(solution)/shard_map/all_gather | solution.py:103
  185.6 12.7 %all_gather.48 = f32[256,256]{0,1:T(8,128)S(1)} all-gather(f32[256,64]{0,1:T(8,128)S(1)} %fusion.17), channel_id=1, replica_groups=mesh['chain'=64,'col'=4] {'col'}, dimensions={1}, use_global_device_ids=true | all-gather | bytes 327680 | tf_op jit(solution)/shard_map/all_gather | solution.py:102
  198.6 11.7 %cholesky.492 = f32[128,128]{1,0:T(8,128)S(1)} custom-call(f32[128,128]{1,0:T(8,128)S(1)} %cholesky.732), custom_call_target="Cholesky" | custom-call | tf_op jit(solution)/shard_map/jit(cholesky)/cholesky | solution.py:20
  210.3 9.8 %custom-call.40 = f32[1,128,128]{1,2,0:T(8,128)S(1)} custom-call(f32[1,128,128]{2,1,0:T(8,128)S(1)} %get-tuple-element.376), custom_call_target="InvertDiagBlocksLowerTriangular" | custom-call | tf_op jit(solution)/shard_map/jit(cholesky)/cholesky | solution.py:20
  220.6 11.7 %cholesky.509 = f32[128,128]{1,0:T(8,128)S(1)} custom-call(f32[128,128]{1,0:T(8,128)S(1)} %convolution_subtract_fusion.22), custom_call_target="Cholesky" | custom-call | tf_op jit(solution)/shard_map/jit(cholesky)/cholesky | solution.py:20
  240.0 19.7 %custom-call.41 = f32[2,128,128]{1,2,0:T(8,128)S(1)} custom-call(f32[2,128,128]{2,1,0:T(8,128)S(1)} %get-tuple-element.220), custom_call_target="InvertDiagBlocksLowerTriangular" | custom-call | tf_op jit(solution)/shard_map/jit(_cho_solve)/triangular_solve | solution.py:22
  276.8 12.2 %all_gather.49 = f32[256,256]{0,1:T(8,128)S(1)} all-gather(f32[256,64]{0,1:T(8,128)S(1)} %convolution_negate_fusion.5), channel_id=1, replica_groups=mesh['chain'=64,'col'=4] {'col'}, dimensions={1}, use_global_device_ids=true | all-gather | bytes 327680 | tf_op jit(solution)/shard_map/all_gather | solution.py:103
  290.3 12.3 %all_gather.50 = f32[256,256]{0,1:T(8,128)S(1)} all-gather(f32[256,64]{0,1:T(8,128)S(1)} %subtract_subtract_fusion.5), channel_id=1, replica_groups=mesh['chain'=64,'col'=4] {'col'}, dimensions={1}, use_global_device_ids=true | all-gather | bytes 327680 | tf_op jit(solution)/shard_map/all_gather | solution.py:102
  302.7 11.7 %cholesky.526 = f32[128,128]{1,0:T(8,128)S(1)} custom-call(f32[128,128]{1,0:T(8,128)S(1)} %cholesky.735), custom_call_target="Cholesky" | custom-call | tf_op jit(solution)/shard_map/jit(cholesky)/cholesky | solution.py:20
  314.5 9.8 %custom-call.42 = f32[1,128,128]{1,2,0:T(8,128)S(1)} custom-call(f32[1,128,128]{2,1,0:T(8,128)S(1)} %get-tuple-element.372), custom_call_target="InvertDiagBlocksLowerTriangular" | custom-call | tf_op jit(solution)/shard_map/jit(cholesky)/cholesky | solution.py:20
  324.8 11.7 %cholesky.543 = f32[128,128]{1,0:T(8,128)S(1)} custom-call(f32[128,128]{1,0:T(8,128)S(1)} %convolution_subtract_fusion.21), custom_call_target="Cholesky" | custom-call | tf_op jit(solution)/shard_map/jit(cholesky)/cholesky | solution.py:20
  344.9 19.7 %custom-call.43 = f32[2,128,128]{1,2,0:T(8,128)S(1)} custom-call(f32[2,128,128]{2,1,0:T(8,128)S(1)} %get-tuple-element.221), custom_call_target="InvertDiagBlocksLowerTriangular" | custom-call | tf_op jit(solution)/shard_map/jit(_cho_solve)/triangular_solve | solution.py:22
  384.7 12.3 %all_gather.51 = f32[256,256]{0,1:T(8,128)S(1)} all-gather(f32[256,64]{0,1:T(8,128)S(1)} %convolution_negate_fusion.4), channel_id=1, replica_groups=mesh['chain'=64,'col'=4] {'col'}, dimensions={1}, use_global_device_ids=true | all-gather | bytes 327680 | tf_op jit(solution)/shard_map/all_gather | solution.py:103
  398.5 12.2 %all_gather.52 = f32[256,256]{0,1:T(8,128)S(1)} all-gather(f32[256,64]{0,1:T(8,128)S(1)} %subtract_subtract_fusion.4), channel_id=1, replica_groups=mesh['chain'=64,'col'=4] {'col'}, dimensions={1}, use_global_device_ids=true | all-gather | bytes 327680 | tf_op jit(solution)/shard_map/all_gather | solution.py:102
  410.9 11.7 %cholesky.560 = f32[128,128]{1,0:T(8,128)S(1)} custom-call(f32[128,128]{1,0:T(8,128)S(1)} %cholesky.738), custom_call_target="Cholesky" | custom-call | tf_op jit(solution)/shard_map/jit(cholesky)/cholesky | solution.py:20
  422.7 9.8 %custom-call.44 = f32[1,128,128]{1,2,0:T(8,128)S(1)} custom-call(f32[1,128,128]{2,1,0:T(8,128)S(1)} %get-tuple-element.368), custom_call_target="InvertDiagBlocksLowerTriangular" | custom-call | tf_op jit(solution)/shard_map/jit(cholesky)/cholesky | solution.py:20
  433.0 11.7 %cholesky.577 = f32[128,128]{1,0:T(8,128)S(1)} custom-call(f32[128,128]{1,0:T(8,128)S(1)} %convolution_subtract_fusion.20), custom_call_target="Cholesky" | custom-call | tf_op jit(solution)/shard_map/jit(cholesky)/cholesky | solution.py:20
  451.8 19.7 %custom-call.45 = f32[2,128,128]{1,2,0:T(8,128)S(1)} custom-call(f32[2,128,128]{2,1,0:T(8,128)S(1)} %get-tuple-element.222), custom_call_target="InvertDiagBlocksLowerTriangular" | custom-call | tf_op jit(solution)/shard_map/jit(_cho_solve)/triangular_solve | solution.py:22
  497.7 12.3 %all_gather.53 = f32[256,256]{0,1:T(8,128)S(1)} all-gather(f32[256,64]{0,1:T(8,128)S(1)} %convolution_negate_fusion.3), channel_id=1, replica_groups=mesh['chain'=64,'col'=4] {'col'}, dimensions={1}, use_global_device_ids=true | all-gather | bytes 327680 | tf_op jit(solution)/shard_map/all_gather | solution.py:103
  511.2 12.3 %all_gather.54 = f32[256,256]{0,1:T(8,128)S(1)} all-gather(f32[256,64]{0,1:T(8,128)S(1)} %subtract_subtract_fusion.3), channel_id=1, replica_groups=mesh['chain'=64,'col'=4] {'col'}, dimensions={1}, use_global_device_ids=true | all-gather | bytes 327680 | tf_op jit(solution)/shard_map/all_gather | solution.py:102
  523.6 11.7 %cholesky.594 = f32[128,128]{1,0:T(8,128)S(1)} custom-call(f32[128,128]{1,0:T(8,128)S(1)} %cholesky.741), custom_call_target="Cholesky" | custom-call | tf_op jit(solution)/shard_map/jit(cholesky)/cholesky | solution.py:20
  545.7 11.7 %cholesky.611 = f32[128,128]{1,0:T(8,128)S(1)} custom-call(f32[128,128]{1,0:T(8,128)S(1)} %convolution_subtract_fusion.19), custom_call_target="Cholesky" | custom-call | tf_op jit(solution)/shard_map/jit(cholesky)/cholesky | solution.py:20
  565.5 19.7 %custom-call.47 = f32[2,128,128]{1,2,0:T(8,128)S(1)} custom-call(f32[2,128,128]{2,1,0:T(8,128)S(1)} %get-tuple-element.223), custom_call_target="InvertDiagBlocksLowerTriangular" | custom-call | tf_op jit(solution)/shard_map/jit(_cho_solve)/triangular_solve | solution.py:22
  606.4 12.2 %all_gather.55 = f32[256,256]{0,1:T(8,128)S(1)} all-gather(f32[256,64]{0,1:T(8,128)S(1)} %convolution_negate_fusion.2), channel_id=1, replica_groups=mesh['chain'=64,'col'=4] {'col'}, dimensions={1}, use_global_device_ids=true | all-gather | bytes 327680 | tf_op jit(solution)/shard_map/all_gather | solution.py:103
  620.1 12.2 %all_gather.56 = f32[256,256]{0,1:T(8,128)S(1)} all-gather(f32[256,64]{0,1:T(8,128)S(1)} %subtract_subtract_fusion.2), channel_id=1, replica_groups=mesh['chain'=64,'col'=4] {'col'}, dimensions={1}, use_global_device_ids=true | all-gather | bytes 327680 | tf_op jit(solution)/shard_map/all_gather | solution.py:102
  632.6 11.7 %cholesky.628 = f32[128,128]{1,0:T(8,128)S(1)} custom-call(f32[128,128]{1,0:T(8,128)S(1)} %cholesky.744), custom_call_target="Cholesky" | custom-call | tf_op jit(solution)/shard_map/jit(cholesky)/cholesky | solution.py:20
  654.6 11.7 %cholesky.645 = f32[128,128]{1,0:T(8,128)S(1)} custom-call(f32[128,128]{1,0:T(8,128)S(1)} %convolution_subtract_fusion.18), custom_call_target="Cholesky" | custom-call | tf_op jit(solution)/shard_map/jit(cholesky)/cholesky | solution.py:20
  673.8 19.7 %custom-call.49 = f32[2,128,128]{1,2,0:T(8,128)S(1)} custom-call(f32[2,128,128]{2,1,0:T(8,128)S(1)} %get-tuple-element.224), custom_call_target="InvertDiagBlocksLowerTriangular" | custom-call | tf_op jit(solution)/shard_map/jit(_cho_solve)/triangular_solve | solution.py:22
  720.7 12.2 %all_gather.57 = f32[256,256]{0,1:T(8,128)S(1)} all-gather(f32[256,64]{0,1:T(8,128)S(1)} %convolution_negate_fusion.1), channel_id=1, replica_groups=mesh['chain'=64,'col'=4] {'col'}, dimensions={1}, use_global_device_ids=true | all-gather | bytes 327680 | tf_op jit(solution)/shard_map/all_gather | solution.py:103
  734.2 12.3 %all_gather.58 = f32[256,256]{0,1:T(8,128)S(1)} all-gather(f32[256,64]{0,1:T(8,128)S(1)} %subtract_subtract_fusion.1), channel_id=1, replica_groups=mesh['chain'=64,'col'=4] {'col'}, dimensions={1}, use_global_device_ids=true | all-gather | bytes 327680 | tf_op jit(solution)/shard_map/all_gather | solution.py:102
  746.6 11.7 %cholesky.662 = f32[128,128]{1,0:T(8,128)S(1)} custom-call(f32[128,128]{1,0:T(8,128)S(1)} %cholesky.747), custom_call_target="Cholesky" | custom-call | tf_op jit(solution)/shard_map/jit(cholesky)/cholesky | solution.py:20
  768.7 11.7 %cholesky.679 = f32[128,128]{1,0:T(8,128)S(1)} custom-call(f32[128,128]{1,0:T(8,128)S(1)} %convolution_subtract_fusion.17), custom_call_target="Cholesky" | custom-call | tf_op jit(solution)/shard_map/jit(cholesky)/cholesky | solution.py:20
  789.2 19.7 %custom-call.51 = f32[2,128,128]{1,2,0:T(8,128)S(1)} custom-call(f32[2,128,128]{2,1,0:T(8,128)S(1)} %get-tuple-element.225), custom_call_target="InvertDiagBlocksLowerTriangular" | custom-call | tf_op jit(solution)/shard_map/jit(_cho_solve)/triangular_solve | solution.py:22
  840.2 12.3 %all_gather.59 = f32[256,256]{0,1:T(8,128)S(1)} all-gather(f32[256,64]{0,1:T(8,128)S(1)} %subtract_subtract_fusion), channel_id=1, replica_groups=mesh['chain'=64,'col'=4] {'col'}, dimensions={1}, use_global_device_ids=true | all-gather | bytes 327680 | tf_op jit(solution)/shard_map/all_gather | solution.py:118
  852.6 11.7 %cholesky.696 = f32[128,128]{1,0:T(8,128)S(1)} custom-call(f32[128,128]{1,0:T(8,128)S(1)} %cholesky.750), custom_call_target="Cholesky" | custom-call | tf_op jit(solution)/shard_map/jit(cholesky)/cholesky | solution.py:119
  864.4 9.8 %custom-call.52 = f32[1,128,128]{1,2,0:T(8,128)S(1)} custom-call(f32[1,128,128]{2,1,0:T(8,128)S(1)} %get-tuple-element.352), custom_call_target="InvertDiagBlocksLowerTriangular" | custom-call | tf_op jit(solution)/shard_map/jit(cholesky)/cholesky | solution.py:119
  874.7 11.7 %cholesky.713 = f32[128,128]{1,0:T(8,128)S(1)} custom-call(f32[128,128]{1,0:T(8,128)S(1)} %convolution_subtract_fusion.16), custom_call_target="Cholesky" | custom-call | tf_op jit(solution)/shard_map/jit(cholesky)/cholesky | solution.py:119
  893.8 19.7 %custom-call.20 = f32[2,128,128]{1,2,0:T(8,128)S(1)} custom-call(f32[2,128,128]{2,1,0:T(8,128)S(1)} %get-tuple-element.175), custom_call_target="InvertDiagBlocksLowerTriangular" | custom-call | tf_op jit(solution)/shard_map/jit(_cho_solve)/triangular_solve | solution.py:119
  (456 shorter events, 317.2 us)
Async XLA Ops:
  0.0 0.9 slice-start
  76.1 0.9 copy-start.19
  133.8 20.0 %copy-start.26 = (s32[2,2]{1,0:T(2,128)}, s32[2,2]{1,0:T(2,128)S(1)}, u32[]{:S(2)}) copy-start(s32[2,2]{1,0:T(2,128)S(1)} %get-tuple-element.999) | copy-start | bytes 52
  158.3 10.2 %collective-permute-start.19 = (f32[16,256]{1,0:T(8,128)}, f32[16,256]{1,0:T(8,128)S(1)}, u32[]{:S(2)}, u32[]{:S(2)}) collective-permute-start(f32[16,256]{1,0:T(8,128)} %convolution_subtract_fusion.29), channel_id=1, source_target_pairs={{4,0},{8,4},{12,8},{16,12},{20,16},{24,20},{28,24},{32,28},{36,32}... | collective-permute-start | bytes 49160 | tf_op jit(solution)/shard_map/ppermute | solution.py:12
  160.6 3.9 copy-start.16
  161.7 20.9 %collective-permute-start = (f32[256,256]{1,0:T(8,128)}, f32[256,256]{1,0:T(8,128)S(1)}, u32[]{:S(2)}, u32[]{:S(2)}) collective-permute-start(f32[256,256]{1,0:T(8,128)} %convolution_add_fusion), channel_id=1, source_target_pairs={{4,0},{8,4},{12,8},{16,12},{20,16},{24,20},{28,24},{32,28},{36,32}... | collective-permute-start | bytes 786440 | tf_op jit(solution)/shard_map/ppermute | solution.py:12
  164.9 2.3 copy-start.17
  165.3 4.6 collective-permute-start.1
  262.1 13.5 %collective-permute-start.21 = (f32[16,256]{1,0:T(8,128)S(1)}, f32[16,256]{1,0:T(8,128)S(1)}, u32[]{:S(2)}, u32[]{:S(2)}) collective-permute-start(f32[16,256]{1,0:T(8,128)S(1)} %fusion.228), channel_id=1, source_target_pairs={{4,0},{8,4},{12,8},{16,12},{20,16},{24,20},{28,24},{32,28},{36,32}... | collective-permute-start | bytes 49160 | tf_op jit(solution)/shard_map/ppermute | solution.py:12
  265.4 10.4 %collective-permute-start.4 = (f32[256,64]{0,1:T(8,128)S(1)}, f32[256,64]{0,1:T(8,128)S(1)}, u32[]{:S(2)}, u32[]{:S(2)}) collective-permute-start(f32[256,64]{0,1:T(8,128)S(1)} %fusion.229), channel_id=1, source_target_pairs={{4,0},{8,4},{12,8},{16,12},{20,16},{24,20},{28,24},{32,28},{36,32}... | collective-permute-start | bytes 196616 | tf_op jit(solution)/shard_map/ppermute | solution.py:12
  268.1 99.2 %collective-permute-start.20 = (f32[16,256]{1,0:T(8,128)}, f32[16,256]{1,0:T(8,128)S(1)}, u32[]{:S(2)}, u32[]{:S(2)}) collective-permute-start(f32[16,256]{1,0:T(8,128)} %fusion.247), channel_id=1, source_target_pairs={{0,4},{4,8},{8,12},{12,16},{16,20},{20,24},{24,28},{28,32},{32,36}... | collective-permute-start | bytes 49160 | tf_op jit(solution)/shard_map/ppermute | solution.py:12
  270.1 19.0 %collective-permute-start.3 = (f32[256,256]{1,0:T(8,128)S(1)}, f32[256,256]{1,0:T(8,128)S(1)}, u32[]{:S(2)}, u32[]{:S(2)}) collective-permute-start(f32[256,256]{1,0:T(8,128)S(1)} %pad_maximum_fusion.3), channel_id=1, source_target_pairs={{4,0},{8,4},{12,8},{16,12},{20,16},{24,20},{28,24},{32,28},{36,32}... | collective-permute-start | bytes 786440 | tf_op jit(solution)/shard_map/ppermute | solution.py:12
  273.7 15.8 %collective-permute-start.2 = (f32[256,64]{0,1:T(8,128)S(1)}, f32[256,64]{0,1:T(8,128)S(1)}, u32[]{:S(2)}, u32[]{:S(2)}) collective-permute-start(f32[256,64]{0,1:T(8,128)S(1)} %fusion.241), channel_id=1, source_target_pairs={{0,4},{4,8},{8,12},{12,16},{16,20},{20,24},{24,28},{28,32},{32,36}... | collective-permute-start | bytes 196616 | tf_op jit(solution)/shard_map/ppermute | solution.py:12
  289.0 0.8 copy-start.7
  366.1 0.8 copy-start.9
  367.9 16.2 %collective-permute-start.23 = (f32[16,256]{1,0:T(8,128)S(1)}, f32[16,256]{1,0:T(8,128)S(1)}, u32[]{:S(2)}, u32[]{:S(2)}) collective-permute-start(f32[16,256]{1,0:T(8,128)S(1)} %fusion.209), channel_id=1, source_target_pairs={{8,0},{12,4},{16,8},{20,12},{24,16},{28,20},{32,24},{36,28},{40,32... | collective-permute-start | bytes 49160 | tf_op jit(solution)/shard_map/ppermute | solution.py:12
  370.8 13.4 %collective-permute-start.22 = (f32[16,256]{1,0:T(8,128)S(1)}, f32[16,256]{1,0:T(8,128)S(1)}, u32[]{:S(2)}, u32[]{:S(2)}) collective-permute-start(f32[16,256]{1,0:T(8,128)S(1)} %fusion.249), channel_id=1, source_target_pairs={{0,8},{4,12},{8,16},{12,20},{16,24},{20,28},{24,32},{28,36},{32,40... | collective-permute-start | bytes 49160 | tf_op jit(solution)/shard_map/ppermute | solution.py:12
  372.5 11.7 %copy-start.22 = (f32[16,256]{1,0:T(8,128)S(1)}, f32[16,256]{1,0:T(8,128)}, u32[]{:S(2)}) copy-start(f32[16,256]{1,0:T(8,128)} %copy-done.21) | copy-start | bytes 49156
  372.5 11.9 %collective-permute-start.7 = (f32[256,64]{0,1:T(8,128)S(1)}, f32[256,64]{0,1:T(8,128)S(1)}, u32[]{:S(2)}, u32[]{:S(2)}) collective-permute-start(f32[256,64]{0,1:T(8,128)S(1)} %fusion.227), channel_id=1, source_target_pairs={{8,0},{12,4},{16,8},{20,12},{24,16},{28,20},{32,24},{36,28},{40,32... | collective-permute-start | bytes 196616 | tf_op jit(solution)/shard_map/ppermute | solution.py:12
  378.2 18.8 %collective-permute-start.6 = (f32[256,256]{1,0:T(8,128)S(1)}, f32[256,256]{1,0:T(8,128)S(1)}, u32[]{:S(2)}, u32[]{:S(2)}) collective-permute-start(f32[256,256]{1,0:T(8,128)S(1)} %pad_maximum_fusion.4), channel_id=1, source_target_pairs={{8,0},{12,4},{16,8},{20,12},{24,16},{28,20},{32,24},{36,28},{40,32... | collective-permute-start | bytes 786440 | tf_op jit(solution)/shard_map/ppermute | solution.py:12
  382.9 14.6 %collective-permute-start.5 = (f32[256,64]{0,1:T(8,128)S(1)}, f32[256,64]{0,1:T(8,128)S(1)}, u32[]{:S(2)}, u32[]{:S(2)}) collective-permute-start(f32[256,64]{0,1:T(8,128)S(1)} %fusion.242), channel_id=1, source_target_pairs={{0,8},{4,12},{8,16},{12,20},{16,24},{20,28},{24,32},{28,36},{32,40... | collective-permute-start | bytes 196616 | tf_op jit(solution)/shard_map/ppermute | solution.py:12
  384.7 12.3 %copy-start.10 = (f32[256,64]{0,1:T(8,128)}, f32[256,64]{0,1:T(8,128)S(1)}, u32[]{:S(2)}) copy-start(f32[256,64]{0,1:T(8,128)S(1)} %convolution_negate_fusion.4) | copy-start | bytes 196612
  473.0 0.8 copy-start.11
  474.5 22.1 %collective-permute-start.25 = (f32[16,256]{1,0:T(8,128)S(1)}, f32[16,256]{1,0:T(8,128)S(1)}, u32[]{:S(2)}, u32[]{:S(2)}) collective-permute-start(f32[16,256]{1,0:T(8,128)S(1)} %fusion.225), channel_id=1, source_target_pairs={{16,0},{20,4},{24,8},{28,12},{32,16},{36,20},{40,24},{44,28},{48,3... | collective-permute-start | bytes 49160 | tf_op jit(solution)/shard_map/ppermute | solution.py:12
  483.0 13.8 %collective-permute-start.10 = (f32[256,64]{0,1:T(8,128)S(1)}, f32[256,64]{0,1:T(8,128)S(1)}, u32[]{:S(2)}, u32[]{:S(2)}) collective-permute-start(f32[256,64]{0,1:T(8,128)S(1)} %fusion.226), channel_id=1, source_target_pairs={{16,0},{20,4},{24,8},{28,12},{32,16},{36,20},{40,24},{44,28},{48,3... | collective-permute-start | bytes 196616 | tf_op jit(solution)/shard_map/ppermute | solution.py:12
  487.9 100.0 %collective-permute-start.24 = (f32[16,256]{1,0:T(8,128)}, f32[16,256]{1,0:T(8,128)S(1)}, u32[]{:S(2)}, u32[]{:S(2)}) collective-permute-start(f32[16,256]{1,0:T(8,128)} %fusion.250), channel_id=1, source_target_pairs={{0,16},{4,20},{8,24},{12,28},{16,32},{20,36},{24,40},{28,44},{32,4... | collective-permute-start | bytes 49160 | tf_op jit(solution)/shard_map/ppermute | solution.py:12
  489.2 20.8 %collective-permute-start.9 = (f32[256,256]{1,0:T(8,128)S(1)}, f32[256,256]{1,0:T(8,128)S(1)}, u32[]{:S(2)}, u32[]{:S(2)}) collective-permute-start(f32[256,256]{1,0:T(8,128)S(1)} %pad_maximum_fusion.5), channel_id=1, source_target_pairs={{16,0},{20,4},{24,8},{28,12},{32,16},{36,20},{40,24},{44,28},{48,3... | collective-permute-start | bytes 786440 | tf_op jit(solution)/shard_map/ppermute | solution.py:12
  495.2 15.2 %collective-permute-start.8 = (f32[256,64]{0,1:T(8,128)S(1)}, f32[256,64]{0,1:T(8,128)S(1)}, u32[]{:S(2)}, u32[]{:S(2)}) collective-permute-start(f32[256,64]{0,1:T(8,128)S(1)} %fusion.243), channel_id=1, source_target_pairs={{0,16},{4,20},{8,24},{12,28},{16,32},{20,36},{24,40},{28,44},{32,4... | collective-permute-start | bytes 196616 | tf_op jit(solution)/shard_map/ppermute | solution.py:12
  588.5 17.3 %collective-permute-start.27 = (f32[16,256]{1,0:T(8,128)S(1)}, f32[16,256]{1,0:T(8,128)S(1)}, u32[]{:S(2)}, u32[]{:S(2)}) collective-permute-start(f32[16,256]{1,0:T(8,128)S(1)} %fusion.210), channel_id=1, source_target_pairs={{32,0},{36,4},{40,8},{44,12},{48,16},{52,20},{56,24},{60,28},{64,3... | collective-permute-start | bytes 49160 | tf_op jit(solution)/shard_map/ppermute | solution.py:12
  594.7 11.2 %collective-permute-start.26 = (f32[16,256]{1,0:T(8,128)S(1)}, f32[16,256]{1,0:T(8,128)S(1)}, u32[]{:S(2)}, u32[]{:S(2)}) collective-permute-start(f32[16,256]{1,0:T(8,128)S(1)} %fusion.252), channel_id=1, source_target_pairs={{0,32},{4,36},{8,40},{12,44},{16,48},{20,52},{24,56},{28,60},{32,6... | collective-permute-start | bytes 49160 | tf_op jit(solution)/shard_map/ppermute | solution.py:12
  596.4 9.5 %copy-start.24 = (f32[16,256]{1,0:T(8,128)S(1)}, f32[16,256]{1,0:T(8,128)}, u32[]{:S(2)}) copy-start(f32[16,256]{1,0:T(8,128)} %copy-done.23) | copy-start | bytes 49156
  596.4 9.7 %collective-permute-start.13 = (f32[256,64]{0,1:T(8,128)S(1)}, f32[256,64]{0,1:T(8,128)S(1)}, u32[]{:S(2)}, u32[]{:S(2)}) collective-permute-start(f32[256,64]{0,1:T(8,128)S(1)} %fusion.224), channel_id=1, source_target_pairs={{32,0},{36,4},{40,8},{44,12},{48,16},{52,20},{56,24},{60,28},{64,3... | collective-permute-start | bytes 196616 | tf_op jit(solution)/shard_map/ppermute | solution.py:12
  601.0 17.7 %collective-permute-start.12 = (f32[256,256]{1,0:T(8,128)S(1)}, f32[256,256]{1,0:T(8,128)S(1)}, u32[]{:S(2)}, u32[]{:S(2)}) collective-permute-start(f32[256,256]{1,0:T(8,128)S(1)} %pad_maximum_fusion.6), channel_id=1, source_target_pairs={{32,0},{36,4},{40,8},{44,12},{48,16},{52,20},{56,24},{60,28},{64,3... | collective-permute-start | bytes 786440 | tf_op jit(solution)/shard_map/ppermute | solution.py:12
  604.5 14.6 %collective-permute-start.11 = (f32[256,64]{0,1:T(8,128)S(1)}, f32[256,64]{0,1:T(8,128)S(1)}, u32[]{:S(2)}, u32[]{:S(2)}) collective-permute-start(f32[256,64]{0,1:T(8,128)S(1)} %fusion.244), channel_id=1, source_target_pairs={{0,32},{4,36},{8,40},{12,44},{16,48},{20,52},{24,56},{28,60},{32,6... | collective-permute-start | bytes 196616 | tf_op jit(solution)/shard_map/ppermute | solution.py:12
  606.4 12.3 %copy-start.14 = (f32[256,64]{0,1:T(8,128)}, f32[256,64]{0,1:T(8,128)S(1)}, u32[]{:S(2)}) copy-start(f32[256,64]{0,1:T(8,128)S(1)} %convolution_negate_fusion.2) | copy-start | bytes 196612
  695.0 0.8 copy-start.15
  696.5 23.1 %collective-permute-start.29 = (f32[16,256]{1,0:T(8,128)S(1)}, f32[16,256]{1,0:T(8,128)S(1)}, u32[]{:S(2)}, u32[]{:S(2)}) collective-permute-start(f32[16,256]{1,0:T(8,128)S(1)} %fusion.222), channel_id=1, source_target_pairs={{64,0},{68,4},{72,8},{76,12},{80,16},{84,20},{88,24},{92,28},{96,3... | collective-permute-start | bytes 49160 | tf_op jit(solution)/shard_map/ppermute | solution.py:12
  706.9 12.9 %collective-permute-start.16 = (f32[256,64]{0,1:T(8,128)S(1)}, f32[256,64]{0,1:T(8,128)S(1)}, u32[]{:S(2)}, u32[]{:S(2)}) collective-permute-start(f32[256,64]{0,1:T(8,128)S(1)} %fusion.223), channel_id=1, source_target_pairs={{64,0},{68,4},{72,8},{76,12},{80,16},{84,20},{88,24},{92,28},{96,3... | collective-permute-start | bytes 196616 | tf_op jit(solution)/shard_map/ppermute | solution.py:12
  711.5 100.1 %collective-permute-start.28 = (f32[16,256]{1,0:T(8,128)}, f32[16,256]{1,0:T(8,128)S(1)}, u32[]{:S(2)}, u32[]{:S(2)}) collective-permute-start(f32[16,256]{1,0:T(8,128)} %fusion.253), channel_id=1, source_target_pairs={{0,64},{4,68},{8,72},{12,76},{16,80},{20,84},{24,88},{28,92},{32,9... | collective-permute-start | bytes 49160 | tf_op jit(solution)/shard_map/ppermute | solution.py:12
  712.8 20.2 %collective-permute-start.15 = (f32[256,256]{1,0:T(8,128)S(1)}, f32[256,256]{1,0:T(8,128)S(1)}, u32[]{:S(2)}, u32[]{:S(2)}) collective-permute-start(f32[256,256]{1,0:T(8,128)S(1)} %pad_maximum_fusion.7), channel_id=1, source_target_pairs={{64,0},{68,4},{72,8},{76,12},{80,16},{84,20},{88,24},{92,28},{96,3... | collective-permute-start | bytes 786440 | tf_op jit(solution)/shard_map/ppermute | solution.py:12
  718.3 15.2 %collective-permute-start.14 = (f32[256,64]{0,1:T(8,128)S(1)}, f32[256,64]{0,1:T(8,128)S(1)}, u32[]{:S(2)}, u32[]{:S(2)}) collective-permute-start(f32[256,64]{0,1:T(8,128)S(1)} %fusion.245), channel_id=1, source_target_pairs={{0,64},{4,68},{8,72},{12,76},{16,80},{20,84},{24,88},{28,92},{32,9... | collective-permute-start | bytes 196616 | tf_op jit(solution)/shard_map/ppermute | solution.py:12
  810.4 0.8 copy-start.5
  811.9 19.1 %collective-permute-start.31 = (f32[16,256]{1,0:T(8,128)S(1)}, f32[16,256]{1,0:T(8,128)S(1)}, u32[]{:S(2)}, u32[]{:S(2)}) collective-permute-start(f32[16,256]{1,0:T(8,128)S(1)} %fusion.211), channel_id=1, source_target_pairs={{128,0},{132,4},{136,8},{140,12},{144,16},{148,20},{152,24},{156,2... | collective-permute-start | bytes 49160 | tf_op jit(solution)/shard_map/ppermute | solution.py:12
  819.5 11.5 %collective-permute-start.30 = (f32[16,256]{1,0:T(8,128)S(1)}, f32[16,256]{1,0:T(8,128)S(1)}, u32[]{:S(2)}, u32[]{:S(2)}) collective-permute-start(f32[16,256]{1,0:T(8,128)S(1)} %fusion.255), channel_id=1, source_target_pairs={{0,128},{4,132},{8,136},{12,140},{16,144},{20,148},{24,152},{28,15... | collective-permute-start | bytes 49160 | tf_op jit(solution)/shard_map/ppermute | solution.py:12
  820.8 12.3 %collective-permute-start.18 = (f32[256,256]{1,0:T(8,128)S(1)}, f32[256,256]{1,0:T(8,128)S(1)}, u32[]{:S(2)}, u32[]{:S(2)}) collective-permute-start(f32[256,256]{1,0:T(8,128)S(1)} %pad_maximum_fusion.8), channel_id=1, source_target_pairs={{128,0},{132,4},{136,8},{140,12},{144,16},{148,20},{152,24},{156,2... | collective-permute-start | bytes 786440 | tf_op jit(solution)/shard_map/ppermute | solution.py:12
  829.7 10.1 %collective-permute-start.17 = (f32[256,64]{0,1:T(8,128)S(1)}, f32[256,64]{0,1:T(8,128)S(1)}, u32[]{:S(2)}, u32[]{:S(2)}) collective-permute-start(f32[256,64]{0,1:T(8,128)S(1)} %fusion.246), channel_id=1, source_target_pairs={{0,128},{4,132},{8,136},{12,140},{16,144},{20,148},{24,152},{28,15... | collective-permute-start | bytes 196616 | tf_op jit(solution)/shard_map/ppermute | solution.py:12
  889.6 23.8 %copy-start.25 = (f32[256,16]{0,1:T(8,128)S(1)}, f32[256,16]{0,1:T(8,128)}, u32[]{:S(2)}) copy-start(f32[256,16]{0,1:T(8,128)} %subtract_bitcast_fusion) | copy-start | bytes 49156
  915.0 5.1 collective-permute-start.32
  (17 other events, 11.6 us)
where the time goes:
time: 934 us; the launch traced here: 924 us
  other arithmetic  490 us (52%)
  blocking collectives  187 us (20%)
  starting transfers between devices  114 us (12%)
  local copies, waits for them, and re-layouts  56.2 us (6%)
  matrix products  47.9 us (5%)
  between operations  13.9 us (1%)
  waiting for transfers between devices  12 us (1%)
    another operation x55, other arithmetic, invert(): lower_factor = jnp.linalg.cholesky(matrix)  276 us
    another operation x23, other arithmetic, invert(): return jax.scipy.linalg.cho_solve((lower_factor, True), identity)  158 us
    ppermute x33, starting transfers between devices, passed_along(): return lax.ppermute(shard, axis, pairs)  114 us
    all_gather x6, blocking collectives, per_device(): lax.all_gather(b_part, 'col', axis=1, tiled=True)  74 us
    all_gather x6, blocking collectives, per_device(): lax.all_gather(c_part, 'col', axis=1, tiled=True)  73.5 us
    another operation x58, local copies, waits for them, and re-layouts, invert(): return jax.scipy.linalg.cho_solve((lower_factor, True), identity)  35.5 us
    another operation x7, other arithmetic, per_device(): jnp.linalg.cholesky(b_final)  34.6 us
    dot_general x71, matrix products, matmul(): return jnp.dot(first_factor, second_factor, precision=finest)  28.7 us
  transfers between devices with their start and end apart: 33, of which 4 were waited for; matrix products, arithmetic and copies ran while one was open for 22% of the time, Pallas kernels for 0%

commit v1 on v0

--- a/solution.py
+++ b/solution.py
@@ -4,6 +4,19 @@
 from jax.sharding import PartitionSpec as P
 
 finest = lax.Precision.HIGHEST
+
+
+def ring_gather(x, axis, dim):
+    ways = lax.axis_size(axis)
+    up = [(d, (d + 1) % ways) for d in range(ways)]
+    down = [(d, (d - 1) % ways) for d in range(ways)]
+    earlier, later = ([x], [x])
+    for _ in range(ways // 2):
+        earlier.append(lax.ppermute(earlier[-1], axis, up))
+    for _ in range((ways - 1) // 2):
+        later.append(lax.ppermute(later[-1], axis, down))
+    line = jnp.concatenate([*earlier[::-1], *later[1:]], axis=dim)
+    return jnp.roll(line, (lax.axis_index(axis) - ways // 2) * x.shape[dim], axis=dim)
 
 
 def passed_along(shard, axis, by):
@@ -99,7 +112,7 @@
     for level_index in range(levels):
         distance = 1 << level_index
         b_full, c_full = (
-            lax.all_gather(b_part, "col", axis=1, tiled=True),
+            ring_gather(b_part, "col", 1),
             lax.all_gather(c_part, "col", axis=1, tiled=True),
         )
         inverse = invert(b_full)

time: 934 us -> 901 us (0.965)
  blocking collectives: 187 us -> 122 us
  waiting for transfers between devices: 12 us -> 47.2 us
    all_gather x6 -> x0, blocking collectives: 74 us -> none  [per_device(): lax.all_gather(b_part, 'col', axis=1, tiled=True)]
    ppermute x33, waiting for transfers between devices: 12 us -> 35.3 us  [passed_along(): return lax.ppermute(shard, axis, pairs)]
    ppermute x33, starting transfers between devices: 114 us -> 95.9 us  [passed_along(): return lax.ppermute(shard, axis, pairs)]
    ppermute x0 -> x18, starting transfers between devices: none -> 14.6 us  [the longest x6 12.3 us: ring_gather(): later.append(lax.ppermute(later[-1], axis, down))]
    ppermute x0 -> x18, waiting for transfers between devices: none -> 11.9 us  [the longest x12 11.9 us: ring_gather(): earlier.append(lax.ppermute(earlier[-1], axis, up))]
  transfers between devices with their start and end apart: 33 -> 51, of which waited for: 4 -> 15; matrix products, arithmetic and copies ran while one was open for 22% -> 23% of each run, Pallas kernels for 0% -> 0%
where the time goes in v1:
time: 901 us; the launch traced here: 885 us
  other arithmetic  493 us (55%)
  blocking collectives  122 us (14%)
  starting transfers between devices  110 us (12%)
  local copies, waits for them, and re-layouts  49.3 us (5%)
  waiting for transfers between devices  47.2 us (5%)
  matrix products  46.5 us (5%)
  between operations  13.8 us (2%)
    another operation x55, other arithmetic, invert(): lower_factor = jnp.linalg.cholesky(matrix)  276 us
    another operation x23, other arithmetic, invert(): return jax.scipy.linalg.cho_solve((lower_factor, True), identity)  158 us
    ppermute x33, starting transfers between devices, passed_along(): return lax.ppermute(shard, axis, pairs)  95.9 us
    all_gather x6, blocking collectives, per_device(): lax.all_gather(c_part, 'col', axis=1, tiled=True)  82.7 us
    ppermute x33, waiting for transfers between devices, passed_along(): return lax.ppermute(shard, axis, pairs)  35.3 us
    another operation x58, local copies, waits for them, and re-layouts, invert(): return jax.scipy.linalg.cho_solve((lower_factor, True), identity)  35 us
    another operation x7, other arithmetic, per_device(): jnp.linalg.cholesky(b_final)  34.7 us
    dot_general x71, matrix products, matmul(): return jnp.dot(first_factor, second_factor, precision=finest)  27.2 us
  transfers between devices with their start and end apart: 51, of which 15 were waited for; matrix products, arithmetic and copies ran while one was open for 23% of the time, Pallas kernels for 0%

profile of v1, /device:TPU:250, one launch (start us, length us, event | category | flops | bytes accessed | tf_op | source)
XLA Modules:
  0.0 885.5 jit_solution(9501200632800768447)
XLA Ops:
  1.0 13.5 %all_gather.27 = f32[2,256,256]{2,0,1:T(2,128)S(1)} all-gather(f32[2,64,256]{2,0,1:T(2,128)S(1)} %copy.26), channel_id=1, replica_groups=mesh['chain'=64,'col'=4] {'col'}, dimensions={1}, use_global_device_ids=true | all-gather | bytes 655360 | tf_op jit(solution)/shard_map/all_gather | solution.py:66
  15.1 11.7 %cholesky.424 = f32[128,128]{1,0:T(8,128)S(1)} custom-call(f32[128,128]{1,0:T(8,128)S(1)} %cholesky.726), custom_call_target="Cholesky" | custom-call | tf_op jit(solution)/shard_map/jit(cholesky)/cholesky | solution.py:33
  26.9 9.8 %custom-call.36 = f32[1,128,128]{1,2,0:T(8,128)S(1)} custom-call(f32[1,128,128]{2,1,0:T(8,128)S(1)} %get-tuple-element.385), custom_call_target="InvertDiagBlocksLowerTriangular" | custom-call | tf_op jit(solution)/shard_map/jit(cholesky)/cholesky | solution.py:33
  37.2 11.7 %cholesky.441 = f32[128,128]{1,0:T(8,128)S(1)} custom-call(f32[128,128]{1,0:T(8,128)S(1)} %convolution_subtract_fusion.24), custom_call_target="Cholesky" | custom-call | tf_op jit(solution)/shard_map/jit(cholesky)/cholesky | solution.py:33
  55.5 19.7 %custom-call.37 = f32[2,128,128]{1,2,0:T(8,128)S(1)} custom-call(f32[2,128,128]{2,1,0:T(8,128)S(1)} %get-tuple-element.219), custom_call_target="InvertDiagBlocksLowerTriangular" | custom-call | tf_op jit(solution)/shard_map/jit(_cho_solve)/triangular_solve | solution.py:35
  77.6 14.0 %all_gather.28 = f32[3,256,256]{2,1,0:T(8,128)S(1)} all-gather(f32[3,64,256]{2,1,0:T(8,128)S(1)} %copy-done.13), channel_id=1, replica_groups=mesh['chain'=64,'col'=4] {'col'}, dimensions={1}, use_global_device_ids=true | all-gather | bytes 983040 | tf_op jit(solution)/shard_map/all_gather | solution.py:67
  93.7 11.7 %cholesky.458 = f32[128,128]{1,0:T(8,128)S(1)} custom-call(f32[128,128]{1,0:T(8,128)S(1)} %cholesky.729), custom_call_target="Cholesky" | custom-call | tf_op jit(solution)/shard_map/while/body/eval_jaxpr/jit(cholesky)/cholesky | solution.py:33
  105.5 9.8 %custom-call.38 = f32[1,128,128]{1,2,0:T(8,128)S(1)} custom-call(f32[1,128,128]{2,1,0:T(8,128)S(1)} %get-tuple-element.381), custom_call_target="InvertDiagBlocksLowerTriangular" | custom-call | tf_op jit(solution)/shard_map/while/body/eval_jaxpr/jit(cholesky)/cholesky | solution.py:33
  115.8 11.7 %cholesky.475 = f32[128,128]{1,0:T(8,128)S(1)} custom-call(f32[128,128]{1,0:T(8,128)S(1)} %convolution_subtract_fusion.23), custom_call_target="Cholesky" | custom-call | tf_op jit(solution)/shard_map/while/body/eval_jaxpr/jit(cholesky)/cholesky | solution.py:33
  134.3 19.7 %custom-call.39 = f32[2,128,128]{1,2,0:T(8,128)S(1)} custom-call(f32[2,128,128]{2,1,0:T(8,128)S(1)} %get-tuple-element.220), custom_call_target="InvertDiagBlocksLowerTriangular" | custom-call | tf_op jit(solution)/shard_map/while/body/eval_jaxpr/jit(_cho_solve)/triangular_solve | solution.py:35
  174.8 13.4 %all_gather.29 = f32[256,256]{0,1:T(8,128)S(1)} all-gather(f32[256,64]{0,1:T(8,128)S(1)} %bitcast.554), channel_id=1, replica_groups=mesh['chain'=64,'col'=4] {'col'}, dimensions={1}, use_global_device_ids=true | all-gather | bytes 327680 | tf_op jit(solution)/shard_map/all_gather | solution.py:116
  188.8 11.7 %cholesky.492 = f32[128,128]{1,0:T(8,128)S(1)} custom-call(f32[128,128]{1,0:T(8,128)S(1)} %cholesky.732), custom_call_target="Cholesky" | custom-call | tf_op jit(solution)/shard_map/jit(cholesky)/cholesky | solution.py:33
  200.6 9.8 %custom-call.40 = f32[1,128,128]{1,2,0:T(8,128)S(1)} custom-call(f32[1,128,128]{2,1,0:T(8,128)S(1)} %get-tuple-element.377), custom_call_target="InvertDiagBlocksLowerTriangular" | custom-call | tf_op jit(solution)/shard_map/jit(cholesky)/cholesky | solution.py:33
  210.9 11.7 %cholesky.509 = f32[128,128]{1,0:T(8,128)S(1)} custom-call(f32[128,128]{1,0:T(8,128)S(1)} %convolution_subtract_fusion.22), custom_call_target="Cholesky" | custom-call | tf_op jit(solution)/shard_map/jit(cholesky)/cholesky | solution.py:33
  230.2 19.7 %custom-call.41 = f32[2,128,128]{1,2,0:T(8,128)S(1)} custom-call(f32[2,128,128]{2,1,0:T(8,128)S(1)} %get-tuple-element.221), custom_call_target="InvertDiagBlocksLowerTriangular" | custom-call | tf_op jit(solution)/shard_map/jit(_cho_solve)/triangular_solve | solution.py:35
  273.6 13.7 %all_gather.30 = f32[256,256]{0,1:T(8,128)S(1)} all-gather(f32[256,64]{0,1:T(8,128)S(1)} %convolution_negate_fusion.5), channel_id=1, replica_groups=mesh['chain'=64,'col'=4] {'col'}, dimensions={1}, use_global_device_ids=true | all-gather | bytes 327680 | tf_op jit(solution)/shard_map/all_gather | solution.py:116
  287.9 11.7 %cholesky.526 = f32[128,128]{1,0:T(8,128)S(1)} custom-call(f32[128,128]{1,0:T(8,128)S(1)} %cholesky.735), custom_call_target="Cholesky" | custom-call | tf_op jit(solution)/shard_map/jit(cholesky)/cholesky | solution.py:33
  299.7 9.8 %custom-call.42 = f32[1,128,128]{1,2,0:T(8,128)S(1)} custom-call(f32[1,128,128]{2,1,0:T(8,128)S(1)} %get-tuple-element.373), custom_call_target="InvertDiagBlocksLowerTriangular" | custom-call | tf_op jit(solution)/shard_map/jit(cholesky)/cholesky | solution.py:33
  310.0 11.7 %cholesky.543 = f32[128,128]{1,0:T(8,128)S(1)} custom-call(f32[128,128]{1,0:T(8,128)S(1)} %convolution_subtract_fusion.21), custom_call_target="Cholesky" | custom-call | tf_op jit(solution)/shard_map/jit(cholesky)/cholesky | solution.py:33
  329.8 19.7 %custom-call.43 = f32[2,128,128]{1,2,0:T(8,128)S(1)} custom-call(f32[2,128,128]{2,1,0:T(8,128)S(1)} %get-tuple-element.222), custom_call_target="InvertDiagBlocksLowerTriangular" | custom-call | tf_op jit(solution)/shard_map/jit(_cho_solve)/triangular_solve | solution.py:35
  380.0 13.8 %all_gather.31 = f32[256,256]{0,1:T(8,128)S(1)} all-gather(f32[256,64]{0,1:T(8,128)S(1)} %convolution_negate_fusion.4), channel_id=1, replica_groups=mesh['chain'=64,'col'=4] {'col'}, dimensions={1}, use_global_device_ids=true | all-gather | bytes 327680 | tf_op jit(solution)/shard_map/all_gather | solution.py:116
  394.5 11.7 %cholesky.560 = f32[128,128]{1,0:T(8,128)S(1)} custom-call(f32[128,128]{1,0:T(8,128)S(1)} %cholesky.738), custom_call_target="Cholesky" | custom-call | tf_op jit(solution)/shard_map/jit(cholesky)/cholesky | solution.py:33
  406.3 9.8 %custom-call.44 = f32[1,128,128]{1,2,0:T(8,128)S(1)} custom-call(f32[1,128,128]{2,1,0:T(8,128)S(1)} %get-tuple-element.369), custom_call_target="InvertDiagBlocksLowerTriangular" | custom-call | tf_op jit(solution)/shard_map/jit(cholesky)/cholesky | solution.py:33
  416.6 11.7 %cholesky.577 = f32[128,128]{1,0:T(8,128)S(1)} custom-call(f32[128,128]{1,0:T(8,128)S(1)} %convolution_subtract_fusion.20), custom_call_target="Cholesky" | custom-call | tf_op jit(solution)/shard_map/jit(cholesky)/cholesky | solution.py:33
  435.5 19.7 %custom-call.45 = f32[2,128,128]{1,2,0:T(8,128)S(1)} custom-call(f32[2,128,128]{2,1,0:T(8,128)S(1)} %get-tuple-element.223), custom_call_target="InvertDiagBlocksLowerTriangular" | custom-call | tf_op jit(solution)/shard_map/jit(_cho_solve)/triangular_solve | solution.py:35
  487.5 14.0 %all_gather.32 = f32[256,256]{0,1:T(8,128)S(1)} all-gather(f32[256,64]{0,1:T(8,128)S(1)} %convolution_negate_fusion.3), channel_id=1, replica_groups=mesh['chain'=64,'col'=4] {'col'}, dimensions={1}, use_global_device_ids=true | all-gather | bytes 327680 | tf_op jit(solution)/shard_map/all_gather | solution.py:116
  502.2 11.7 %cholesky.594 = f32[128,128]{1,0:T(8,128)S(1)} custom-call(f32[128,128]{1,0:T(8,128)S(1)} %cholesky.741), custom_call_target="Cholesky" | custom-call | tf_op jit(solution)/shard_map/jit(cholesky)/cholesky | solution.py:33
  514.0 9.8 %custom-call.46 = f32[1,128,128]{1,2,0:T(8,128)S(1)} custom-call(f32[1,128,128]{2,1,0:T(8,128)S(1)} %get-tuple-element.365), custom_call_target="InvertDiagBlocksLowerTriangular" | custom-call | tf_op jit(solution)/shard_map/jit(cholesky)/cholesky | solution.py:33
  524.3 11.7 %cholesky.611 = f32[128,128]{1,0:T(8,128)S(1)} custom-call(f32[128,128]{1,0:T(8,128)S(1)} %convolution_subtract_fusion.19), custom_call_target="Cholesky" | custom-call | tf_op jit(solution)/shard_map/jit(cholesky)/cholesky | solution.py:33
  544.3 19.7 %custom-call.47 = f32[2,128,128]{1,2,0:T(8,128)S(1)} custom-call(f32[2,128,128]{2,1,0:T(8,128)S(1)} %get-tuple-element.224), custom_call_target="InvertDiagBlocksLowerTriangular" | custom-call | tf_op jit(solution)/shard_map/jit(_cho_solve)/triangular_solve | solution.py:35
  593.5 13.9 %all_gather.33 = f32[256,256]{0,1:T(8,128)S(1)} all-gather(f32[256,64]{0,1:T(8,128)S(1)} %convolution_negate_fusion.2), channel_id=1, replica_groups=mesh['chain'=64,'col'=4] {'col'}, dimensions={1}, use_global_device_ids=true | all-gather | bytes 327680 | tf_op jit(solution)/shard_map/all_gather | solution.py:116
  608.1 11.7 %cholesky.628 = f32[128,128]{1,0:T(8,128)S(1)} custom-call(f32[128,128]{1,0:T(8,128)S(1)} %cholesky.744), custom_call_target="Cholesky" | custom-call | tf_op jit(solution)/shard_map/jit(cholesky)/cholesky | solution.py:33
  619.8 9.8 %custom-call.48 = f32[1,128,128]{1,2,0:T(8,128)S(1)} custom-call(f32[1,128,128]{2,1,0:T(8,128)S(1)} %get-tuple-element.361), custom_call_target="InvertDiagBlocksLowerTriangular" | custom-call | tf_op jit(solution)/shard_map/jit(cholesky)/cholesky | solution.py:33
  630.1 11.7 %cholesky.645 = f32[128,128]{1,0:T(8,128)S(1)} custom-call(f32[128,128]{1,0:T(8,128)S(1)} %convolution_subtract_fusion.18), custom_call_target="Cholesky" | custom-call | tf_op jit(solution)/shard_map/jit(cholesky)/cholesky | solution.py:33
  649.1 19.7 %custom-call.49 = f32[2,128,128]{1,2,0:T(8,128)S(1)} custom-call(f32[2,128,128]{2,1,0:T(8,128)S(1)} %get-tuple-element.225), custom_call_target="InvertDiagBlocksLowerTriangular" | custom-call | tf_op jit(solution)/shard_map/jit(_cho_solve)/triangular_solve | solution.py:35
  684.7 6.4 collective-permute-done.29
  696.1 13.9 %all_gather.34 = f32[256,256]{0,1:T(8,128)S(1)} all-gather(f32[256,64]{0,1:T(8,128)S(1)} %convolution_negate_fusion.1), channel_id=1, replica_groups=mesh['chain'=64,'col'=4] {'col'}, dimensions={1}, use_global_device_ids=true | all-gather | bytes 327680 | tf_op jit(solution)/shard_map/all_gather | solution.py:116
  710.6 11.7 %cholesky.662 = f32[128,128]{1,0:T(8,128)S(1)} custom-call(f32[128,128]{1,0:T(8,128)S(1)} %cholesky.747), custom_call_target="Cholesky" | custom-call | tf_op jit(solution)/shard_map/jit(cholesky)/cholesky | solution.py:33
  722.4 9.8 %custom-call.50 = f32[1,128,128]{1,2,0:T(8,128)S(1)} custom-call(f32[1,128,128]{2,1,0:T(8,128)S(1)} %get-tuple-element.357), custom_call_target="InvertDiagBlocksLowerTriangular" | custom-call | tf_op jit(solution)/shard_map/jit(cholesky)/cholesky | solution.py:33
  732.7 11.7 %cholesky.679 = f32[128,128]{1,0:T(8,128)S(1)} custom-call(f32[128,128]{1,0:T(8,128)S(1)} %convolution_subtract_fusion.17), custom_call_target="Cholesky" | custom-call | tf_op jit(solution)/shard_map/jit(cholesky)/cholesky | solution.py:33
  752.5 19.7 %custom-call.51 = f32[2,128,128]{1,2,0:T(8,128)S(1)} custom-call(f32[2,128,128]{2,1,0:T(8,128)S(1)} %get-tuple-element.226), custom_call_target="InvertDiagBlocksLowerTriangular" | custom-call | tf_op jit(solution)/shard_map/jit(_cho_solve)/triangular_solve | solution.py:35
  782.4 8.5 collective-permute-start.36
  795.2 6.3 collective-permute-done.35
  801.9 12.3 %all_gather.35 = f32[256,256]{0,1:T(8,128)S(1)} all-gather(f32[256,64]{0,1:T(8,128)S(1)} %subtract_subtract_fusion), channel_id=1, replica_groups=mesh['chain'=64,'col'=4] {'col'}, dimensions={1}, use_global_device_ids=true | all-gather | bytes 327680 | tf_op jit(solution)/shard_map/all_gather | solution.py:131
  814.4 11.7 %cholesky.696 = f32[128,128]{1,0:T(8,128)S(1)} custom-call(f32[128,128]{1,0:T(8,128)S(1)} %cholesky.750), custom_call_target="Cholesky" | custom-call | tf_op jit(solution)/shard_map/jit(cholesky)/cholesky | solution.py:132
  826.1 9.8 %custom-call.52 = f32[1,128,128]{1,2,0:T(8,128)S(1)} custom-call(f32[1,128,128]{2,1,0:T(8,128)S(1)} %get-tuple-element.353), custom_call_target="InvertDiagBlocksLowerTriangular" | custom-call | tf_op jit(solution)/shard_map/jit(cholesky)/cholesky | solution.py:132
  836.4 11.7 %cholesky.713 = f32[128,128]{1,0:T(8,128)S(1)} custom-call(f32[128,128]{1,0:T(8,128)S(1)} %convolution_subtract_fusion.16), custom_call_target="Cholesky" | custom-call | tf_op jit(solution)/shard_map/jit(cholesky)/cholesky | solution.py:132
  855.7 19.7 %custom-call.20 = f32[2,128,128]{1,2,0:T(8,128)S(1)} custom-call(f32[2,128,128]{2,1,0:T(8,128)S(1)} %get-tuple-element.176), custom_call_target="InvertDiagBlocksLowerTriangular" | custom-call | tf_op jit(solution)/shard_map/jit(_cho_solve)/triangular_solve | solution.py:132
  (480 shorter events, 293.0 us)
Async XLA Ops:
  158.1 9.5 %collective-permute-start.37 = (f32[16,256]{1,0:T(8,128)S(1)}, f32[16,256]{1,0:T(8,128)S(1)}, u32[]{:S(2)}, u32[]{:S(2)}) collective-permute-start(f32[16,256]{1,0:T(8,128)S(1)} %convolution_subtract_fusion.29), channel_id=1, source_target_pairs={{4,0},{8,4},{12,8},{16,12},{20,16},{24,20},{28,24},{32,28},{36,32}... | collective-permute-start | bytes 49160 | tf_op jit(solution)/shard_map/ppermute | solution.py:25
  161.6 6.9 collective-permute-start
  165.2 5.0 collective-permute-start.1
  170.6 17.5 %collective-permute-start.4 = (f32[256,64]{0,1:T(8,128)S(1)}, f32[256,64]{0,1:T(8,128)S(1)}, u32[]{:S(2)}, u32[]{:S(2)}) collective-permute-start(f32[256,64]{0,1:T(8,128)S(1)} %fusion.17), channel_id=1, source_target_pairs={{0,3},{1,0},{2,1},{3,2},{4,7},{5,4},{6,5},{7,6},{8,11},{9,8},{10,9... | collective-permute-start | bytes 196616 | tf_op jit(solution)/shard_map/ppermute | solution.py:17
  174.5 13.7 %collective-permute-start.3 = (f32[256,64]{0,1:T(8,128)S(1)}, f32[256,64]{0,1:T(8,128)S(1)}, u32[]{:S(2)}, u32[]{:S(2)}) collective-permute-start(f32[256,64]{0,1:T(8,128)S(1)} %collective-permute-done.2), channel_id=1, source_target_pairs={{0,1},{1,2},{2,3},{3,0},{4,5},{5,6},{6,7},{7,4},{8,9},{9,10},{10,1... | collective-permute-start | bytes 196616 | tf_op jit(solution)/shard_map/ppermute | solution.py:15
  252.3 12.0 %collective-permute-start.39 = (f32[16,256]{1,0:T(8,128)S(1)}, f32[16,256]{1,0:T(8,128)S(1)}, u32[]{:S(2)}, u32[]{:S(2)}) collective-permute-start(f32[16,256]{1,0:T(8,128)S(1)} %fusion.268), channel_id=1, source_target_pairs={{4,0},{8,4},{12,8},{16,12},{20,16},{24,20},{28,24},{32,28},{36,32}... | collective-permute-start | bytes 49160 | tf_op jit(solution)/shard_map/ppermute | solution.py:25
  254.3 10.3 %collective-permute-start.6 = (f32[256,256]{1,0:T(8,128)S(1)}, f32[256,256]{1,0:T(8,128)S(1)}, u32[]{:S(2)}, u32[]{:S(2)}) collective-permute-start(f32[256,256]{1,0:T(8,128)S(1)} %pad_maximum_fusion.3), channel_id=1, source_target_pairs={{4,0},{8,4},{12,8},{16,12},{20,16},{24,20},{28,24},{32,28},{36,32}... | collective-permute-start | bytes 786440 | tf_op jit(solution)/shard_map/ppermute | solution.py:25
  258.1 10.6 %collective-permute-start.7 = (f32[256,64]{0,1:T(8,128)S(1)}, f32[256,64]{0,1:T(8,128)S(1)}, u32[]{:S(2)}, u32[]{:S(2)}) collective-permute-start(f32[256,64]{0,1:T(8,128)S(1)} %fusion.269), channel_id=1, source_target_pairs={{4,0},{8,4},{12,8},{16,12},{20,16},{24,20},{28,24},{32,28},{36,32}... | collective-permute-start | bytes 196616 | tf_op jit(solution)/shard_map/ppermute | solution.py:25
  260.0 92.2 %collective-permute-start.38 = (f32[16,256]{1,0:T(8,128)}, f32[16,256]{1,0:T(8,128)S(1)}, u32[]{:S(2)}, u32[]{:S(2)}) collective-permute-start(f32[16,256]{1,0:T(8,128)} %fusion.287), channel_id=1, source_target_pairs={{0,4},{4,8},{8,12},{12,16},{16,20},{20,24},{24,28},{28,32},{32,36}... | collective-permute-start | bytes 49160 | tf_op jit(solution)/shard_map/ppermute | solution.py:25
  262.4 5.6 collective-permute-start.5
  268.4 5.0 collective-permute-start.8
  269.0 18.3 %collective-permute-start.10 = (f32[256,64]{0,1:T(8,128)S(1)}, f32[256,64]{0,1:T(8,128)S(1)}, u32[]{:S(2)}, u32[]{:S(2)}) collective-permute-start(f32[256,64]{0,1:T(8,128)S(1)} %subtract_subtract_fusion.5), channel_id=1, source_target_pairs={{0,3},{1,0},{2,1},{3,2},{4,7},{5,4},{6,5},{7,6},{8,11},{9,8},{10,9... | collective-permute-start | bytes 196616 | tf_op jit(solution)/shard_map/ppermute | solution.py:17
  273.4 13.9 %collective-permute-start.9 = (f32[256,64]{0,1:T(8,128)S(1)}, f32[256,64]{0,1:T(8,128)S(1)}, u32[]{:S(2)}, u32[]{:S(2)}) collective-permute-start(f32[256,64]{0,1:T(8,128)S(1)} %collective-permute-done.8), channel_id=1, source_target_pairs={{0,1},{1,2},{2,3},{3,0},{4,5},{5,6},{6,7},{7,4},{8,9},{9,10},{10,1... | collective-permute-start | bytes 196616 | tf_op jit(solution)/shard_map/ppermute | solution.py:15
  352.9 17.3 %collective-permute-start.41 = (f32[16,256]{1,0:T(8,128)S(1)}, f32[16,256]{1,0:T(8,128)S(1)}, u32[]{:S(2)}, u32[]{:S(2)}) collective-permute-start(f32[16,256]{1,0:T(8,128)S(1)} %fusion.249), channel_id=1, source_target_pairs={{8,0},{12,4},{16,8},{20,12},{24,16},{28,20},{32,24},{36,28},{40,32... | collective-permute-start | bytes 49160 | tf_op jit(solution)/shard_map/ppermute | solution.py:25
  357.0 13.1 %collective-permute-start.40 = (f32[16,256]{1,0:T(8,128)S(1)}, f32[16,256]{1,0:T(8,128)S(1)}, u32[]{:S(2)}, u32[]{:S(2)}) collective-permute-start(f32[16,256]{1,0:T(8,128)S(1)} %fusion.289), channel_id=1, source_target_pairs={{0,8},{4,12},{8,16},{12,20},{16,24},{20,28},{24,32},{28,36},{32,40... | collective-permute-start | bytes 49160 | tf_op jit(solution)/shard_map/ppermute | solution.py:25
  358.3 12.1 %collective-permute-start.12 = (f32[256,256]{1,0:T(8,128)S(1)}, f32[256,256]{1,0:T(8,128)S(1)}, u32[]{:S(2)}, u32[]{:S(2)}) collective-permute-start(f32[256,256]{1,0:T(8,128)S(1)} %pad_maximum_fusion.4), channel_id=1, source_target_pairs={{8,0},{12,4},{16,8},{20,12},{24,16},{28,20},{32,24},{36,28},{40,32... | collective-permute-start | bytes 786440 | tf_op jit(solution)/shard_map/ppermute | solution.py:25
  363.4 12.1 %collective-permute-start.13 = (f32[256,64]{0,1:T(8,128)S(1)}, f32[256,64]{0,1:T(8,128)S(1)}, u32[]{:S(2)}, u32[]{:S(2)}) collective-permute-start(f32[256,64]{0,1:T(8,128)S(1)} %fusion.267), channel_id=1, source_target_pairs={{8,0},{12,4},{16,8},{20,12},{24,16},{28,20},{32,24},{36,28},{40,32... | collective-permute-start | bytes 196616 | tf_op jit(solution)/shard_map/ppermute | solution.py:25
  368.8 6.2 collective-permute-start.11
  375.8 18.1 %collective-permute-start.16 = (f32[256,64]{0,1:T(8,128)S(1)}, f32[256,64]{0,1:T(8,128)S(1)}, u32[]{:S(2)}, u32[]{:S(2)}) collective-permute-start(f32[256,64]{0,1:T(8,128)S(1)} %subtract_subtract_fusion.4), channel_id=1, source_target_pairs={{0,3},{1,0},{2,1},{3,2},{4,7},{5,4},{6,5},{7,6},{8,11},{9,8},{10,9... | collective-permute-start | bytes 196616 | tf_op jit(solution)/shard_map/ppermute | solution.py:17
  379.7 14.1 %collective-permute-start.15 = (f32[256,64]{0,1:T(8,128)S(1)}, f32[256,64]{0,1:T(8,128)S(1)}, u32[]{:S(2)}, u32[]{:S(2)}) collective-permute-start(f32[256,64]{0,1:T(8,128)S(1)} %collective-permute-done.14), channel_id=1, source_target_pairs={{0,1},{1,2},{2,3},{3,0},{4,5},{5,6},{6,7},{7,4},{8,9},{9,10},{10,1... | collective-permute-start | bytes 196616 | tf_op jit(solution)/shard_map/ppermute | solution.py:15
  457.6 17.9 %collective-permute-start.43 = (f32[16,256]{1,0:T(8,128)S(1)}, f32[16,256]{1,0:T(8,128)S(1)}, u32[]{:S(2)}, u32[]{:S(2)}) collective-permute-start(f32[16,256]{1,0:T(8,128)S(1)} %fusion.265), channel_id=1, source_target_pairs={{16,0},{20,4},{24,8},{28,12},{32,16},{36,20},{40,24},{44,28},{48,3... | collective-permute-start | bytes 49160 | tf_op jit(solution)/shard_map/ppermute | solution.py:25
  463.8 12.0 %collective-permute-start.18 = (f32[256,256]{1,0:T(8,128)S(1)}, f32[256,256]{1,0:T(8,128)S(1)}, u32[]{:S(2)}, u32[]{:S(2)}) collective-permute-start(f32[256,256]{1,0:T(8,128)S(1)} %pad_maximum_fusion.5), channel_id=1, source_target_pairs={{16,0},{20,4},{24,8},{28,12},{32,16},{36,20},{40,24},{44,28},{48,3... | collective-permute-start | bytes 786440 | tf_op jit(solution)/shard_map/ppermute | solution.py:25
  467.6 15.4 %collective-permute-start.19 = (f32[256,64]{0,1:T(8,128)S(1)}, f32[256,64]{0,1:T(8,128)S(1)}, u32[]{:S(2)}, u32[]{:S(2)}) collective-permute-start(f32[256,64]{0,1:T(8,128)S(1)} %fusion.266), channel_id=1, source_target_pairs={{16,0},{20,4},{24,8},{28,12},{32,16},{36,20},{40,24},{44,28},{48,3... | collective-permute-start | bytes 196616 | tf_op jit(solution)/shard_map/ppermute | solution.py:25
  472.9 93.8 %collective-permute-start.42 = (f32[16,256]{1,0:T(8,128)}, f32[16,256]{1,0:T(8,128)S(1)}, u32[]{:S(2)}, u32[]{:S(2)}) collective-permute-start(f32[16,256]{1,0:T(8,128)} %fusion.290), channel_id=1, source_target_pairs={{0,16},{4,20},{8,24},{12,28},{16,32},{20,36},{24,40},{28,44},{32,4... | collective-permute-start | bytes 49160 | tf_op jit(solution)/shard_map/ppermute | solution.py:25
  474.2 8.3 collective-permute-start.17
  482.9 4.3 collective-permute-start.20
  483.3 18.3 %collective-permute-start.22 = (f32[256,64]{0,1:T(8,128)S(1)}, f32[256,64]{0,1:T(8,128)S(1)}, u32[]{:S(2)}, u32[]{:S(2)}) collective-permute-start(f32[256,64]{0,1:T(8,128)S(1)} %subtract_subtract_fusion.3), channel_id=1, source_target_pairs={{0,3},{1,0},{2,1},{3,2},{4,7},{5,4},{6,5},{7,6},{8,11},{9,8},{10,9... | collective-permute-start | bytes 196616 | tf_op jit(solution)/shard_map/ppermute | solution.py:17
  487.3 14.3 %collective-permute-start.21 = (f32[256,64]{0,1:T(8,128)S(1)}, f32[256,64]{0,1:T(8,128)S(1)}, u32[]{:S(2)}, u32[]{:S(2)}) collective-permute-start(f32[256,64]{0,1:T(8,128)S(1)} %collective-permute-done.20), channel_id=1, source_target_pairs={{0,1},{1,2},{2,3},{3,0},{4,5},{5,6},{6,7},{7,4},{8,9},{9,10},{10,1... | collective-permute-start | bytes 196616 | tf_op jit(solution)/shard_map/ppermute | solution.py:15
  567.4 16.3 %collective-permute-start.45 = (f32[16,256]{1,0:T(8,128)S(1)}, f32[16,256]{1,0:T(8,128)S(1)}, u32[]{:S(2)}, u32[]{:S(2)}) collective-permute-start(f32[16,256]{1,0:T(8,128)S(1)} %fusion.250), channel_id=1, source_target_pairs={{32,0},{36,4},{40,8},{44,12},{48,16},{52,20},{56,24},{60,28},{64,3... | collective-permute-start | bytes 49160 | tf_op jit(solution)/shard_map/ppermute | solution.py:25
  572.3 11.4 %collective-permute-start.44 = (f32[16,256]{1,0:T(8,128)S(1)}, f32[16,256]{1,0:T(8,128)S(1)}, u32[]{:S(2)}, u32[]{:S(2)}) collective-permute-start(f32[16,256]{1,0:T(8,128)S(1)} %fusion.292), channel_id=1, source_target_pairs={{0,32},{4,36},{8,40},{12,44},{16,48},{20,52},{24,56},{28,60},{32,6... | collective-permute-start | bytes 49160 | tf_op jit(solution)/shard_map/ppermute | solution.py:25
  573.6 10.3 %collective-permute-start.24 = (f32[256,256]{1,0:T(8,128)S(1)}, f32[256,256]{1,0:T(8,128)S(1)}, u32[]{:S(2)}, u32[]{:S(2)}) collective-permute-start(f32[256,256]{1,0:T(8,128)S(1)} %pad_maximum_fusion.6), channel_id=1, source_target_pairs={{32,0},{36,4},{40,8},{44,12},{48,16},{52,20},{56,24},{60,28},{64,3... | collective-permute-start | bytes 786440 | tf_op jit(solution)/shard_map/ppermute | solution.py:25
  578.5 10.5 %collective-permute-start.25 = (f32[256,64]{0,1:T(8,128)S(1)}, f32[256,64]{0,1:T(8,128)S(1)}, u32[]{:S(2)}, u32[]{:S(2)}) collective-permute-start(f32[256,64]{0,1:T(8,128)S(1)} %fusion.264), channel_id=1, source_target_pairs={{32,0},{36,4},{40,8},{44,12},{48,16},{52,20},{56,24},{60,28},{64,3... | collective-permute-start | bytes 196616 | tf_op jit(solution)/shard_map/ppermute | solution.py:25
  582.4 6.2 collective-permute-start.23
  588.9 4.3 collective-permute-start.26
  589.3 18.1 %collective-permute-start.28 = (f32[256,64]{0,1:T(8,128)S(1)}, f32[256,64]{0,1:T(8,128)S(1)}, u32[]{:S(2)}, u32[]{:S(2)}) collective-permute-start(f32[256,64]{0,1:T(8,128)S(1)} %subtract_subtract_fusion.2), channel_id=1, source_target_pairs={{0,3},{1,0},{2,1},{3,2},{4,7},{5,4},{6,5},{7,6},{8,11},{9,8},{10,9... | collective-permute-start | bytes 196616 | tf_op jit(solution)/shard_map/ppermute | solution.py:17
  593.3 14.1 %collective-permute-start.27 = (f32[256,64]{0,1:T(8,128)S(1)}, f32[256,64]{0,1:T(8,128)S(1)}, u32[]{:S(2)}, u32[]{:S(2)}) collective-permute-start(f32[256,64]{0,1:T(8,128)S(1)} %collective-permute-done.26), channel_id=1, source_target_pairs={{0,1},{1,2},{2,3},{3,0},{4,5},{5,6},{6,7},{7,4},{8,9},{9,10},{10,1... | collective-permute-start | bytes 196616 | tf_op jit(solution)/shard_map/ppermute | solution.py:15
  671.3 12.7 %collective-permute-start.47 = (f32[16,256]{1,0:T(8,128)S(1)}, f32[16,256]{1,0:T(8,128)S(1)}, u32[]{:S(2)}, u32[]{:S(2)}) collective-permute-start(f32[16,256]{1,0:T(8,128)S(1)} %fusion.262), channel_id=1, source_target_pairs={{64,0},{68,4},{72,8},{76,12},{80,16},{84,20},{88,24},{92,28},{96,3... | collective-permute-start | bytes 49160 | tf_op jit(solution)/shard_map/ppermute | solution.py:25
  675.9 8.3 collective-permute-start.30
  679.5 12.1 %collective-permute-start.31 = (f32[256,64]{0,1:T(8,128)S(1)}, f32[256,64]{0,1:T(8,128)S(1)}, u32[]{:S(2)}, u32[]{:S(2)}) collective-permute-start(f32[256,64]{0,1:T(8,128)S(1)} %fusion.263), channel_id=1, source_target_pairs={{64,0},{68,4},{72,8},{76,12},{80,16},{84,20},{88,24},{92,28},{96,3... | collective-permute-start | bytes 196616 | tf_op jit(solution)/shard_map/ppermute | solution.py:25
  681.4 93.5 %collective-permute-start.46 = (f32[16,256]{1,0:T(8,128)}, f32[16,256]{1,0:T(8,128)S(1)}, u32[]{:S(2)}, u32[]{:S(2)}) collective-permute-start(f32[16,256]{1,0:T(8,128)} %fusion.293), channel_id=1, source_target_pairs={{0,64},{4,68},{8,72},{12,76},{16,80},{20,84},{24,88},{28,92},{32,9... | collective-permute-start | bytes 49160 | tf_op jit(solution)/shard_map/ppermute | solution.py:25
  682.7 8.4 collective-permute-start.29
  691.8 18.1 %collective-permute-start.34 = (f32[256,64]{0,1:T(8,128)S(1)}, f32[256,64]{0,1:T(8,128)S(1)}, u32[]{:S(2)}, u32[]{:S(2)}) collective-permute-start(f32[256,64]{0,1:T(8,128)S(1)} %subtract_subtract_fusion.1), channel_id=1, source_target_pairs={{0,3},{1,0},{2,1},{3,2},{4,7},{5,4},{6,5},{7,6},{8,11},{9,8},{10,9... | collective-permute-start | bytes 196616 | tf_op jit(solution)/shard_map/ppermute | solution.py:17
  695.8 14.2 %collective-permute-start.33 = (f32[256,64]{0,1:T(8,128)S(1)}, f32[256,64]{0,1:T(8,128)S(1)}, u32[]{:S(2)}, u32[]{:S(2)}) collective-permute-start(f32[256,64]{0,1:T(8,128)S(1)} %collective-permute-done.32), channel_id=1, source_target_pairs={{0,1},{1,2},{2,3},{3,0},{4,5},{5,6},{6,7},{7,4},{8,9},{9,10},{10,1... | collective-permute-start | bytes 196616 | tf_op jit(solution)/shard_map/ppermute | solution.py:15
  775.2 17.4 %collective-permute-start.49 = (f32[16,256]{1,0:T(8,128)S(1)}, f32[16,256]{1,0:T(8,128)S(1)}, u32[]{:S(2)}, u32[]{:S(2)}) collective-permute-start(f32[16,256]{1,0:T(8,128)S(1)} %fusion.251), channel_id=1, source_target_pairs={{128,0},{132,4},{136,8},{140,12},{144,16},{148,20},{152,24},{156,2... | collective-permute-start | bytes 49160 | tf_op jit(solution)/shard_map/ppermute | solution.py:25
  781.1 11.5 %collective-permute-start.48 = (f32[16,256]{1,0:T(8,128)S(1)}, f32[16,256]{1,0:T(8,128)S(1)}, u32[]{:S(2)}, u32[]{:S(2)}) collective-permute-start(f32[16,256]{1,0:T(8,128)S(1)} %fusion.295), channel_id=1, source_target_pairs={{0,128},{4,132},{8,136},{12,140},{16,144},{20,148},{24,152},{28,15... | collective-permute-start | bytes 49160 | tf_op jit(solution)/shard_map/ppermute | solution.py:25
  782.4 12.3 %collective-permute-start.36 = (f32[256,256]{1,0:T(8,128)S(1)}, f32[256,256]{1,0:T(8,128)S(1)}, u32[]{:S(2)}, u32[]{:S(2)}) collective-permute-start(f32[256,256]{1,0:T(8,128)S(1)} %pad_maximum_fusion.8), channel_id=1, source_target_pairs={{128,0},{132,4},{136,8},{140,12},{144,16},{148,20},{152,24},{156,2... | collective-permute-start | bytes 786440 | tf_op jit(solution)/shard_map/ppermute | solution.py:25
  791.3 10.2 %collective-permute-start.35 = (f32[256,64]{0,1:T(8,128)S(1)}, f32[256,64]{0,1:T(8,128)S(1)}, u32[]{:S(2)}, u32[]{:S(2)}) collective-permute-start(f32[256,64]{0,1:T(8,128)S(1)} %fusion.286), channel_id=1, source_target_pairs={{0,128},{4,132},{8,136},{12,140},{16,144},{20,148},{24,152},{28,15... | collective-permute-start | bytes 196616 | tf_op jit(solution)/shard_map/ppermute | solution.py:25
  876.9 5.1 collective-permute-start.50
  (29 other events, 219.7 us)
